TPU v7x, 256 devices: a whole 4x4x8 slice. The times are simulated.
256 devices in a mesh: seq: 64 (over y, x, z_hi, core), chan: 4 (over z_lo).
Axes of the slice: x: 4, y: 4, z: 8 (z_hi: 2, z_lo: 4; z = z_hi * 4 + z_lo), core: 2. Of those that a mesh axis runs over, the one named last changes fastest.
Arguments:
- tokens: bfloat16 [512, 768, 1024], P('seq', 'chan'), may hold values from -24 to 24, as said below
- filter_gain: bfloat16 [512, 768, 1024], P('seq', 'chan'), may hold values from -4 to 4
- row_factor: bfloat16 [1024, 1024], replicated, may hold values from -0.1875 to 0.1875
- col_factor: bfloat16 [512, 512], replicated, may hold values from -0.25 to 0.25
- up_weight: bfloat16 [4, 192, 768], P('chan'), may hold values from -0.4375 to 0.4375
- down_weight: bfloat16 [4, 192, 768], P('chan'), may hold values from -0.21875 to 0.21875
Outputs:
- layer_out: bfloat16 [512, 768, 1024], P('seq', 'chan')
Inputs may be any that keep to these rules, and one draw needn't show every extreme that they name: `tokens`: layer activations.
All inputs are finite; a program needn't handle non-finite values.
Results may differ from a plain program's by a relative error of at most 0.0075.
Values may be sent and summed in bfloat16 or wider, within the bound.
A program may use at most 128 MiB of HBM per device.

v0:
```python
import jax
import jax.numpy as jnp
from jax import lax
from jax.sharding import PartitionSpec as P

D = 768


def finish(source, mixed, up_weight, down_weight):
    src = source.astype(jnp.float32)
    gated = src + mixed.astype(jnp.float32) * jax.nn.sigmoid(src)
    total = lax.psum(jnp.sum(gated, axis=1), "chan")
    mean = total / D
    centered = gated - mean[:, None, :]
    spread = lax.psum(jnp.sum(centered * centered, axis=1), "chan") / D
    normed = (centered * lax.rsqrt(spread + 1e-05)[:, None, :]).astype(jnp.bfloat16)
    hidden = jax.nn.gelu(
        jnp.einsum("xky,kh->xhy", normed, up_weight[0], preferred_element_type=jnp.float32)
    ).astype(jnp.bfloat16)
    back = jnp.einsum("xhy,kh->xky", hidden, down_weight[0], preferred_element_type=jnp.float32)
    return (gated + back).astype(jnp.bfloat16)


def body(tokens, filter_gain, row_factor, col_factor, up_weight, down_weight):
    spun = jnp.einsum("rck,bk->rcb", tokens, row_factor, preferred_element_type=jnp.float32)
    filtered = (filter_gain.astype(jnp.float32) * spun).astype(jnp.bfloat16)
    by_channel = jnp.transpose(filtered, (1, 0, 2))
    owned = lax.all_to_all(by_channel, "seq", split_axis=0, concat_axis=1, tiled=True)
    mixed = jnp.einsum("ak,ckb->cab", col_factor, owned, preferred_element_type=jnp.float32)
    back = lax.all_to_all(
        mixed.astype(jnp.bfloat16), "seq", split_axis=1, concat_axis=0, tiled=True
    )
    return finish(tokens, jnp.transpose(back, (1, 0, 2)), up_weight, down_weight)


def solution(mesh):
    return jax.shard_map(
        body,
        mesh=mesh,
        in_specs=(
            P("seq", "chan", None),
            P("seq", "chan", None),
            P(),
            P(),
            P("chan", None, None),
            P("chan", None, None),
        ),
        out_specs=P("seq", "chan", None),
        check_vma=False,
    )
```

profile of v0, /device:TPU:2, one launch (start us, length us, event | category | flops | bytes accessed | tf_op | source)
XLA Modules:
  0.0 280.5 jit_solution(5488151017067106785)
XLA Ops:
  0.0 0.0 copy-start
  0.0 1.6 copy-done
  1.6 6.1 %fusion.17 = bf16[192,8,1024]{2,0,1:T(8,128)(2,1)S(1)} fusion(bf16[8,192,1024]{2,1,0:T(8,128)(2,1)} %param.7, bf16[8,192,1024]{2,1,0:T(8,128)(2,1)} %param.6, bf16[1024,1024]{1,0:T(8,128)(2,1)S(1)} %copy-done), kind=kOutput, calls=%fused_computation.23 | convolution fusion | flops 3225944064 | bytes 11534336 | tf_op jit(solution)/shard_map/rck,bk->rcb/dot_general | solution.py:25
  7.7 0.0 copy-start.2
  7.7 1.7 copy.17
  9.4 91.3 %all_to_all.27 = bf16[192,8,1024]{2,1,0:T(8,128)(2,1)S(1)} all-to-all(bf16[192,8,1024]{2,1,0:T(8,128)(2,1)S(1)} %copy.17), channel_id=1, replica_groups=mesh['seq'=64,'chan'=4] {'seq'}, dimensions={0} | all-to-all | bytes 6291456 | tf_op jit(solution)/shard_map/all_to_all | solution.py:28
  100.7 0.0 copy-done.2
  100.7 3.5 %convert_bitcast_fusion.1 = bf16[3,512,1024]{1,2,0:T(8,128)(2,1)} fusion(bf16[3,64,8,1024]{3,2,0,1:T(8,128)(2,1)S(1)} %bitcast.47, bf16[512,512]{1,0:T(8,128)(2,1)S(1)} %copy-done.2), kind=kOutput, calls=%fused_computation.29 | convolution fusion | flops 1612185600 | bytes 6815744 | tf_op jit(solution)/shard_map/ak,ckb->cab/dot_general | solution.py:29
  104.2 7.8 %copy.20 = bf16[3,512,1024]{2,0,1:T(4,128)(2,1)} copy(bf16[3,512,1024]{1,2,0:T(8,128)(2,1)} %convert_bitcast_fusion.1) | data formatting | bytes 6291456 | tf_op jit(solution)/shard_map/convert_element_type | solution.py:31
  112.0 71.4 %all_to_all.28 = bf16[3,512,1024]{2,0,1:T(4,128)(2,1)S(1)} all-to-all(bf16[3,512,1024]{2,0,1:T(4,128)(2,1)} %copy.20), channel_id=1, replica_groups=mesh['seq'=64,'chan'=4] {'seq'}, dimensions={1} | all-to-all | bytes 6291456 | tf_op jit(solution)/shard_map/all_to_all | solution.py:30
  183.4 1.4 convert_bitcast_fusion
  184.7 0.0 copy-start.1
  184.7 1.1 copy.22
  185.9 0.8 copy-done.1
  186.6 8.3 %fusion.38 = (f32[8,1024]{1,0:T(8,128)S(1)}, f32[8,192,1024]{2,1,0:T(8,128)}) fusion(f32[192,8,1024]{2,1,0:T(8,128)S(1)} %bitcast.46, bf16[8,192,1024]{2,1,0:T(8,128)(2,1)S(1)} %copy-done.1), kind=kLoop, calls=%fused_computation.40 | loop fusion | flops 11001856 | bytes 15761408 | tf_op jit(solution)/shard_map/reduce_sum | solution.py:12
  194.9 0.0 copy-start.3
  194.9 0.0 copy-start.4
  194.9 51.1 %psum.14 = f32[8,1024]{1,0:T(8,128)S(1)} all-reduce(f32[8,1024]{1,0:T(8,128)S(1)} %get-tuple-element.5), channel_id=1, replica_groups=mesh['seq'=64,'chan'=4] {'chan'}, use_global_device_ids=true, to_apply=%region_1.0 | all-reduce | flops 8192 | bytes 65536 | tf_op jit(solution)/shard_map/psum | solution.py:12
  246.0 3.7 %multiply_reduce_fusion = f32[8,1024]{1,0:T(8,128)S(1)} fusion(f32[8,192,1024]{2,1,0:T(8,128)} %get-tuple-element.6, f32[8,1024]{1,0:T(8,128)S(1)} %broadcast_multiply_fusion), kind=kLoop, calls=%fused_computation.21 | loop fusion | flops 4710400 | bytes 6356992 | tf_op jit(solution)/shard_map/reduce_sum | solution.py:15
  249.7 16.0 %psum.15 = f32[8,1024]{1,0:T(8,128)S(1)} all-reduce(f32[8,1024]{1,0:T(8,128)S(1)} %multiply_reduce_fusion), channel_id=1, replica_groups=mesh['seq'=64,'chan'=4] {'chan'}, use_global_device_ids=true, to_apply=%region_3.0 | all-reduce | flops 8192 | bytes 65536 | tf_op jit(solution)/shard_map/psum | solution.py:15
  265.7 0.0 copy-done.3
  265.7 0.0 copy-done.4
  265.7 14.8 %fusion.16 = bf16[8,192,1024]{2,1,0:T(8,128)(2,1)} fusion(f32[8,192,1024]{2,1,0:T(8,128)} %get-tuple-element.6, f32[8,1024]{1,0:T(8,128)S(1)} %add_rsqrt_fusion, f32[8,1024]{1,0:T(8,128)S(1)} %broadcast_multiply_fusion, bf16[1,192,768]{2,1,0:T(8,128)(2,1)S(1)} %copy-done.3, bf16[1,192,768]{2,1,0:T(8,128)(2,1)S(1)} %copy-done.4), kind=kOutput, calls=%fused_computation.19 | convolution fusion | flops 4896325632 | bytes 10092544 | tf_op jit(solution)/shard_map/xhy,kh->xky/dot_general | solution.py:20
  (2 shorter events, 0.0 us)
Async XLA Ops:
  0.0 1.6 copy-start
  7.7 93.0 %copy-start.2 = (bf16[512,512]{1,0:T(8,128)(2,1)S(1)}, bf16[512,512]{1,0:T(8,128)(2,1)}, u32[]{:S(2)}) copy-start(bf16[512,512]{1,0:T(8,128)(2,1)} %param.9) | copy-start | bytes 1572868
  184.7 1.9 copy-start.1
  194.9 70.8 %copy-start.3 = (bf16[1,192,768]{2,1,0:T(8,128)(2,1)S(1)}, bf16[1,192,768]{2,1,0:T(8,128)(2,1)}, u32[]{:S(2)}) copy-start(bf16[1,192,768]{2,1,0:T(8,128)(2,1)} %param.11) | copy-start | bytes 884740
  194.9 70.8 %copy-start.4 = (bf16[1,192,768]{2,1,0:T(8,128)(2,1)S(1)}, bf16[1,192,768]{2,1,0:T(8,128)(2,1)}, u32[]{:S(2)}) copy-start(bf16[1,192,768]{2,1,0:T(8,128)(2,1)} %param.10) | copy-start | bytes 884740
where the time goes:
time: 281 us
  blocking collectives  230 us (82%)
  matrix products  24.4 us (9%)
  other arithmetic  13.3 us (5%)
  local copies, waits for them, and re-layouts  13 us (5%)
    all_to_all x1, blocking collectives, body(): lax.all_to_all(by_channel, 'seq', split_axis=0, concat_axis=1, tiled=True)  91.3 us
    all_to_all x1, blocking collectives, body(): lax.all_to_all(mixed.astype(jnp.bfloat16), 'seq', split_axis=1, concat_ax...  71.4 us
    psum x1, blocking collectives, finish(): total = lax.psum(jnp.sum(gated, axis=1), 'chan')  51.1 us
    psum x1, blocking collectives, finish(): spread = lax.psum(jnp.sum(centered * centered, axis=1), 'chan') / D  16 us
    dot_general x1, matrix products, finish(): jnp.einsum('xhy,kh->xky', hidden, down_weight[0], preferred_element_type=...  14.8 us
    reduce_sum x1, other arithmetic, finish(): total = lax.psum(jnp.sum(gated, axis=1), 'chan')  8.29 us
    convert_element_type x1, local copies, waits for them, and re-layouts, body(): mixed.astype(jnp.bfloat16)  7.78 us
    dot_general x1, matrix products, body(): jnp.einsum('rck,bk->rcb', tokens, row_factor, preferred_element_type=jnp....  6.08 us

commit v1 on v0

--- a/solution.py
+++ b/solution.py
@@ -25,7 +25,10 @@
     spun = jnp.einsum("rck,bk->rcb", tokens, row_factor, preferred_element_type=jnp.float32)
     filtered = (filter_gain.astype(jnp.float32) * spun).astype(jnp.bfloat16)
     by_channel = jnp.transpose(filtered, (1, 0, 2))
-    owned = lax.all_to_all(by_channel, "seq", split_axis=0, concat_axis=1, tiled=True)
+    owned = jnp.concatenate(
+        lax.all_to_all(jnp.stack(jnp.split(by_channel, lax.axis_size("seq"), axis=0)), "seq", 0, 0),
+        axis=1,
+    )
     mixed = jnp.einsum("ak,ckb->cab", col_factor, owned, preferred_element_type=jnp.float32)
     back = lax.all_to_all(
         mixed.astype(jnp.bfloat16), "seq", split_axis=1, concat_axis=0, tiled=True

time: 281 us -> 284 us (1.011)
  local copies, waits for them, and re-layouts: 13 us -> 16.2 us
    unnamed x10 -> x73, local copies, waits for them, and re-layouts: 2.37 us -> 5.49 us
where the time goes in v1:
time: 284 us
  blocking collectives  230 us (81%)
  matrix products  24.4 us (9%)
  local copies, waits for them, and re-layouts  16.2 us (6%)
  other arithmetic  13.3 us (5%)
    all_to_all x1, blocking collectives, body(): lax.all_to_all(jnp.stack(jnp.split(by_channel, lax.axis_size('seq'), axis...  91.4 us
    all_to_all x1, blocking collectives, body(): lax.all_to_all(mixed.astype(jnp.bfloat16), 'seq', split_axis=1, concat_ax...  71.4 us
    psum x1, blocking collectives, finish(): total = lax.psum(jnp.sum(gated, axis=1), 'chan')  51.1 us
    psum x1, blocking collectives, finish(): spread = lax.psum(jnp.sum(centered * centered, axis=1), 'chan') / D  16 us
    dot_general x1, matrix products, finish(): jnp.einsum('xhy,kh->xky', hidden, down_weight[0], preferred_element_type=...  14.8 us
    reduce_sum x1, other arithmetic, finish(): total = lax.psum(jnp.sum(gated, axis=1), 'chan')  8.29 us
    convert_element_type x1, local copies, waits for them, and re-layouts, body(): mixed.astype(jnp.bfloat16)  7.78 us
    dot_general x1, matrix products, body(): jnp.einsum('rck,bk->rcb', tokens, row_factor, preferred_element_type=jnp....  6.08 us

profile of v1, /device:TPU:2, one launch (start us, length us, event | category | flops | bytes accessed | tf_op | source)
XLA Modules:
  0.0 283.9 jit_solution(4160892861983925364)
XLA Ops:
  0.0 1.6 copy-done
  1.6 6.1 %fusion.17 = bf16[192,8,1024]{2,0,1:T(8,128)(2,1)S(1)} fusion(bf16[8,192,1024]{2,1,0:T(8,128)(2,1)} %param.7, bf16[8,192,1024]{2,1,0:T(8,128)(2,1)} %param.6, bf16[1024,1024]{1,0:T(8,128)(2,1)S(1)} %copy-done), kind=kOutput, calls=%fused_computation.23 | convolution fusion | flops 3225944064 | bytes 11534336 | tf_op jit(solution)/shard_map/rck,bk->rcb/dot_general | solution.py:25
  7.8 0.1 constant_dynamic-update-slice_fusion.61
  7.9 0.1 constant_dynamic-update-slice_fusion.58
  8.2 0.1 constant_dynamic-update-slice_fusion.53
  8.3 0.1 constant_dynamic-update-slice_fusion.50
  8.6 0.1 constant_dynamic-update-slice_fusion.45
  8.7 0.1 constant_dynamic-update-slice_fusion.42
  9.0 0.1 constant_dynamic-update-slice_fusion.37
  9.2 0.1 constant_dynamic-update-slice_fusion.34
  9.4 0.1 constant_dynamic-update-slice_fusion.29
  11.0 1.7 copy.22
  12.7 91.4 %all_to_all.14 = bf16[64,3,8,1024]{3,2,1,0:T(8,128)(2,1)S(1)} all-to-all(bf16[64,3,8,1024]{3,2,1,0:T(8,128)(2,1)S(1)} %copy.22), channel_id=1, replica_groups=mesh['seq'=64,'chan'=4] {'seq'}, dimensions={0} | all-to-all | bytes 6291456 | tf_op jit(solution)/shard_map/all_to_all | solution.py:29
  104.1 3.5 %convert_bitcast_fusion.1 = bf16[3,512,1024]{1,2,0:T(8,128)(2,1)} fusion(bf16[64,3,8,1024]{3,2,1,0:T(8,128)(2,1)S(1)} %all_to_all.14, bf16[512,512]{1,0:T(8,128)(2,1)S(1)} %copy-done.2), kind=kOutput, calls=%fused_computation.29 | convolution fusion | flops 1612185600 | bytes 6815744 | tf_op jit(solution)/shard_map/ak,ckb->cab/dot_general | solution.py:32
  107.6 7.8 %copy.25 = bf16[3,512,1024]{2,0,1:T(4,128)(2,1)} copy(bf16[3,512,1024]{1,2,0:T(8,128)(2,1)} %convert_bitcast_fusion.1) | data formatting | bytes 6291456 | tf_op jit(solution)/shard_map/convert_element_type | solution.py:34
  115.4 71.4 %all_to_all.15 = bf16[3,512,1024]{2,0,1:T(4,128)(2,1)S(1)} all-to-all(bf16[3,512,1024]{2,0,1:T(4,128)(2,1)} %copy.25), channel_id=1, replica_groups=mesh['seq'=64,'chan'=4] {'seq'}, dimensions={1} | all-to-all | bytes 6291456 | tf_op jit(solution)/shard_map/all_to_all | solution.py:33
  186.8 1.4 convert_bitcast_fusion
  188.2 1.1 copy.27
  189.3 0.8 copy-done.1
  190.0 8.3 %fusion.38 = (f32[8,1024]{1,0:T(8,128)S(1)}, f32[8,192,1024]{2,1,0:T(8,128)}) fusion(f32[192,8,1024]{2,1,0:T(8,128)S(1)} %bitcast.301, bf16[8,192,1024]{2,1,0:T(8,128)(2,1)S(1)} %copy-done.1), kind=kLoop, calls=%fused_computation.168 | loop fusion | flops 11001856 | bytes 15761408 | tf_op jit(solution)/shard_map/reduce_sum | solution.py:12
  198.3 51.1 %psum.14 = f32[8,1024]{1,0:T(8,128)S(1)} all-reduce(f32[8,1024]{1,0:T(8,128)S(1)} %get-tuple-element.5), channel_id=1, replica_groups=mesh['seq'=64,'chan'=4] {'chan'}, use_global_device_ids=true, to_apply=%region_1.0 | all-reduce | flops 8192 | bytes 65536 | tf_op jit(solution)/shard_map/psum | solution.py:12
  249.4 3.7 %multiply_reduce_fusion = f32[8,1024]{1,0:T(8,128)S(1)} fusion(f32[8,192,1024]{2,1,0:T(8,128)} %get-tuple-element.6, f32[8,1024]{1,0:T(8,128)S(1)} %broadcast_multiply_fusion), kind=kLoop, calls=%fused_computation.21 | loop fusion | flops 4710400 | bytes 6356992 | tf_op jit(solution)/shard_map/reduce_sum | solution.py:15
  253.1 16.0 %psum.15 = f32[8,1024]{1,0:T(8,128)S(1)} all-reduce(f32[8,1024]{1,0:T(8,128)S(1)} %multiply_reduce_fusion), channel_id=1, replica_groups=mesh['seq'=64,'chan'=4] {'chan'}, use_global_device_ids=true, to_apply=%region_3.0 | all-reduce | flops 8192 | bytes 65536 | tf_op jit(solution)/shard_map/psum | solution.py:15
  269.1 14.8 %fusion.16 = bf16[8,192,1024]{2,1,0:T(8,128)(2,1)} fusion(f32[8,192,1024]{2,1,0:T(8,128)} %get-tuple-element.6, f32[8,1024]{1,0:T(8,128)S(1)} %add_rsqrt_fusion, f32[8,1024]{1,0:T(8,128)S(1)} %broadcast_multiply_fusion, bf16[1,192,768]{2,1,0:T(8,128)(2,1)S(1)} %copy-done.3, bf16[1,192,768]{2,1,0:T(8,128)(2,1)S(1)} %copy-done.4), kind=kOutput, calls=%fused_computation.19 | convolution fusion | flops 4896325632 | bytes 10092544 | tf_op jit(solution)/shard_map/xhy,kh->xky/dot_general | solution.py:20
  (65 shorter events, 2.7 us)
Async XLA Ops:
  0.0 1.6 copy-start
  12.7 91.4 %copy-start.2 = (bf16[512,512]{1,0:T(8,128)(2,1)S(1)}, bf16[512,512]{1,0:T(8,128)(2,1)}, u32[]{:S(2)}) copy-start(bf16[512,512]{1,0:T(8,128)(2,1)} %param.9) | copy-start | bytes 1572868
  188.1 1.9 copy-start.1
  198.3 70.8 %copy-start.3 = (bf16[1,192,768]{2,1,0:T(8,128)(2,1)S(1)}, bf16[1,192,768]{2,1,0:T(8,128)(2,1)}, u32[]{:S(2)}) copy-start(bf16[1,192,768]{2,1,0:T(8,128)(2,1)} %param.11) | copy-start | bytes 884740
  198.3 70.8 %copy-start.4 = (bf16[1,192,768]{2,1,0:T(8,128)(2,1)S(1)}, bf16[1,192,768]{2,1,0:T(8,128)(2,1)}, u32[]{:S(2)}) copy-start(bf16[1,192,768]{2,1,0:T(8,128)(2,1)} %param.10) | copy-start | bytes 884740
